TPU v7x, 32 devices: a whole 2x2x4 slice. The times are simulated.
32 devices in a mesh: fsdp: 8 (over z, y), seq: 4 (over x, core).
Axes of the slice: x: 2, y: 2, z: 4, core: 2. Of those that a mesh axis runs over, the one named last changes fastest.
Arguments:
- frames_in: bfloat16 [16, 1536, 1280], P('fsdp', 'seq'), may hold values from -6 to 6
- teacher: bfloat16 [16, 1536, 1280], P('fsdp', 'seq'), may hold values from -6 to 6
- lengths: int32 [16], replicated, may hold values from 384 to 1536, as said below
- norm1_gain: bfloat16 [1280], P('fsdp'), may hold values from 0.25 to 1.75
- norm1_bias: bfloat16 [1280], P('fsdp'), may hold values from -1.75 to 1.75
- w_qkv: bfloat16 [1280, 3840], P('fsdp'), may hold values from -0.15625 to 0.15625
- query_bias: bfloat16 [1280], P('fsdp'), may hold values from -1.75 to 1.75
- value_bias: bfloat16 [1280], P('fsdp'), may hold values from -1.75 to 1.75
- w_attn_out: bfloat16 [1280, 1280], P('fsdp'), may hold values from -0.875 to 0.875
- attn_out_bias: bfloat16 [1280], P('fsdp'), may hold values from -1.75 to 1.75
- norm2_gain: bfloat16 [1280], P('fsdp'), may hold values from 0.25 to 1.75
- norm2_bias: bfloat16 [1280], P('fsdp'), may hold values from -1.75 to 1.75
- w_up: bfloat16 [1280, 5120], P('fsdp'), may hold values from -0.15625 to 0.15625
- up_bias: bfloat16 [5120], P('fsdp'), may hold values from -1.75 to 1.75
- w_down: bfloat16 [5120, 1280], P('fsdp'), may hold values from -0.125 to 0.125
- down_bias: bfloat16 [1280], P('fsdp'), may hold values from -1.75 to 1.75
Outputs:
- frames_out: bfloat16 [16, 1536, 1280], P('fsdp', 'seq')
- clip_loss: float32 [16], P('fsdp')
- grad_in: float32 [16, 1536, 1280], P('fsdp', 'seq')
- grad_norm1_gain: float32 [1280], P('fsdp')
- grad_norm1_bias: float32 [1280], P('fsdp')
- grad_w_qkv: float32 [1280, 3840], P('fsdp')
- grad_query_bias: float32 [1280], P('fsdp')
- grad_value_bias: float32 [1280], P('fsdp')
- grad_w_attn_out: float32 [1280, 1280], P('fsdp')
- grad_attn_out_bias: float32 [1280], P('fsdp')
- grad_norm2_gain: float32 [1280], P('fsdp')
- grad_norm2_bias: float32 [1280], P('fsdp')
- grad_w_up: float32 [1280, 5120], P('fsdp')
- grad_up_bias: float32 [5120], P('fsdp')
- grad_w_down: float32 [5120, 1280], P('fsdp')
- grad_down_bias: float32 [1280], P('fsdp')
Inputs may be any that keep to these rules, and one draw needn't show every extreme that they name: `lengths`: a clip's valid frames are its first ones; in every draw some clip has all 1536 frames valid.
All inputs are finite; a program needn't handle non-finite values.
Results may differ from a plain program's by a relative error of at most 0.0095.
Values may be sent and summed in bfloat16 or wider, within the bound.
A program may use at most 256 MiB of HBM per device.

v0:
```python
import functools
import math
import jax
import jax.numpy as jnp
from jax import lax
from jax.sharding import PartitionSpec as P

HEADS = 16


def layer_norm(v, gain, bias):
    mean = jnp.mean(v, axis=-1, keepdims=True)
    cent = v - mean
    var = jnp.mean(cent * cent, axis=-1, keepdims=True)
    return cent * lax.rsqrt(var + 1e-05) * gain + bias


def local(
    frames_in,
    teacher,
    lengths,
    norm1_gain,
    norm1_bias,
    w_qkv,
    query_bias,
    value_bias,
    w_attn_out,
    attn_out_bias,
    norm2_gain,
    norm2_bias,
    w_up,
    up_bias,
    w_down,
    down_bias,
):
    single = jnp.float32
    half = jnp.bfloat16
    gain1, bias1, wqkv, qbias, vbias, wout, obias, gain2, bias2, wup, ubias, wdown, dbias = (
        lax.all_gather(norm1_gain, "fsdp", axis=0, tiled=True),
        lax.all_gather(norm1_bias, "fsdp", axis=0, tiled=True),
        lax.all_gather(w_qkv, "fsdp", axis=0, tiled=True),
        lax.all_gather(query_bias, "fsdp", axis=0, tiled=True),
        lax.all_gather(value_bias, "fsdp", axis=0, tiled=True),
        lax.all_gather(w_attn_out, "fsdp", axis=0, tiled=True),
        lax.all_gather(attn_out_bias, "fsdp", axis=0, tiled=True),
        lax.all_gather(norm2_gain, "fsdp", axis=0, tiled=True),
        lax.all_gather(norm2_bias, "fsdp", axis=0, tiled=True),
        lax.all_gather(w_up, "fsdp", axis=0, tiled=True),
        lax.all_gather(up_bias, "fsdp", axis=0, tiled=True),
        lax.all_gather(w_down, "fsdp", axis=0, tiled=True),
        lax.all_gather(down_bias, "fsdp", axis=0, tiled=True),
    )
    clips, frames, width = frames_in.shape
    groups = lax.axis_size("seq")
    seq_len = frames * groups
    head_dim = width // HEADS
    local_heads = HEADS // groups
    span = local_heads * head_dim
    rows = clips * frames
    block = min(512, seq_len)
    nblocks = seq_len // block
    scale = 1.0 / math.sqrt(head_dim)
    mine = lax.dynamic_slice_in_dim(lengths, lax.axis_index("fsdp") * clips, clips)
    place = lax.axis_index("seq") * frames + jnp.arange(frames, dtype=jnp.int32)
    row_valid = (place[None, :] < mine[:, None]).astype(single)
    key_valid = jnp.arange(seq_len, dtype=jnp.int32)[None, :] < mine[:, None]
    state = frames_in.astype(single).reshape(rows, width)
    hidden1, norm1_back = jax.vjp(layer_norm, state, gain1.astype(single), bias1.astype(single))
    hidden1 = hidden1.astype(half)
    qkv = jnp.dot(hidden1, wqkv, preferred_element_type=single)
    query = (qkv[:, :width] + qbias.astype(single)).astype(half)
    keyed = qkv[:, width : 2 * width].astype(half)
    valued = (qkv[:, 2 * width :] + vbias.astype(single)).astype(half)

    def to_groups(tensor):
        return tensor.reshape(clips, frames, groups, span)

    query_h, keyed_h, valued_h = (
        lax.all_to_all(to_groups(query), "seq", split_axis=2, concat_axis=1, tiled=True),
        lax.all_to_all(to_groups(keyed), "seq", split_axis=2, concat_axis=1, tiled=True),
        lax.all_to_all(to_groups(valued), "seq", split_axis=2, concat_axis=1, tiled=True),
    )
    query_h = query_h.reshape(clips, seq_len, local_heads, head_dim)
    keyed_h = keyed_h.reshape(clips, seq_len, local_heads, head_dim)
    valued_h = valued_h.reshape(clips, seq_len, local_heads, head_dim)

    def scores_of(query_block, keys, valid):
        scores = (
            jnp.einsum("qhd,khd->hqk", query_block, keys, preferred_element_type=single) * scale
        )
        return jnp.where(valid[None, None, :], scores, -1e30)

    def attend(item):
        queries, keys, values, valid = item
        blocks = queries.reshape(nblocks, block, local_heads, head_dim)

        def one_block(query_block):
            scores = scores_of(query_block, keys, valid)
            top = jnp.max(scores, axis=-1, keepdims=True)
            expo = jnp.exp(scores - top)
            total = jnp.sum(expo, axis=-1, keepdims=True)
            probs = (expo / total).astype(half)
            context = jnp.einsum("hqk,khd->qhd", probs, values, preferred_element_type=single)
            return (context.astype(half), (top + jnp.log(total))[..., 0])

        context, logsum = lax.map(one_block, blocks)
        return (context.reshape(seq_len, span), logsum)

    context_h, logsum = lax.map(attend, (query_h, keyed_h, valued_h, key_valid))
    context = lax.all_to_all(
        context_h.reshape(clips, seq_len, 1, span), "seq", split_axis=1, concat_axis=2, tiled=True
    ).reshape(rows, width)
    attn = jnp.dot(context, wout, preferred_element_type=single) + obias.astype(single)
    middle = state + attn
    hidden2, norm2_back = jax.vjp(layer_norm, middle, gain2.astype(single), bias2.astype(single))
    hidden2 = hidden2.astype(half)
    upper = jnp.dot(hidden2, wup, preferred_element_type=single) + ubias.astype(single)
    active, gelu_back = jax.vjp(functools.partial(jax.nn.gelu, approximate=False), upper)
    active = active.astype(half)
    result = middle + jnp.dot(active, wdown, preferred_element_type=single) + dbias.astype(single)
    frames_out = result.astype(half).reshape(clips, frames, width)
    count = jnp.sum(lengths).astype(single)
    diff = (result - teacher.astype(single).reshape(rows, width)).reshape(clips, frames, width)
    masked = diff * row_valid[:, :, None]
    part_loss = jnp.sum(masked * diff, axis=(1, 2)) / (2.0 * width * count)
    grad_out = (masked * (float(lengths.shape[0] * seq_len) / count)).reshape(rows, width)
    wqkv_b, wout_b, wup_b, wdown_b = (
        lax.all_gather(w_qkv, "fsdp", axis=0, tiled=True),
        lax.all_gather(w_attn_out, "fsdp", axis=0, tiled=True),
        lax.all_gather(w_up, "fsdp", axis=0, tiled=True),
        lax.all_gather(w_down, "fsdp", axis=0, tiled=True),
    )
    grad_branch2 = grad_out.astype(half)
    grad_wdown = jnp.dot(active.T, grad_branch2, preferred_element_type=single)
    grad_dbias = jnp.sum(grad_branch2.astype(single), axis=0)
    grad_active = jnp.dot(grad_branch2, wdown_b.T, preferred_element_type=single)
    (grad_upper,) = gelu_back(grad_active)
    grad_upper = grad_upper.astype(half)
    grad_wup = jnp.dot(hidden2.T, grad_upper, preferred_element_type=single)
    grad_ubias = jnp.sum(grad_upper.astype(single), axis=0)
    grad_hidden2 = jnp.dot(grad_upper, wup_b.T, preferred_element_type=single)
    grad_middle_norm, grad_gain2, grad_bias2 = norm2_back(grad_hidden2)
    grad_middle = grad_out + grad_middle_norm
    grad_branch1 = grad_middle.astype(half)
    grad_wout = jnp.dot(context.T, grad_branch1, preferred_element_type=single)
    grad_obias = jnp.sum(grad_branch1.astype(single), axis=0)
    grad_context = jnp.dot(grad_branch1, wout_b.T, preferred_element_type=single).astype(half)
    grad_context_h = lax.all_to_all(
        grad_context.reshape(clips, frames, groups, span),
        "seq",
        split_axis=2,
        concat_axis=1,
        tiled=True,
    )
    grad_context_h = grad_context_h.reshape(clips, seq_len, local_heads, head_dim)

    def attend_back(item):
        queries, keys, values, grads, sums, valid = item
        query_blocks = queries.reshape(nblocks, block, local_heads, head_dim)
        grad_blocks = grads.reshape(nblocks, block, local_heads, head_dim)

        def one_block(carry, piece):
            query_block, grad_block, sum_block = piece
            scores = scores_of(query_block, keys, valid)
            probs = jnp.exp(scores - sum_block[..., None])
            grad_probs = jnp.einsum(
                "qhd,khd->hqk", grad_block, values, preferred_element_type=single
            )
            inner = jnp.sum(probs * grad_probs, axis=-1, keepdims=True)
            grad_scores = (probs * (grad_probs - inner)).astype(half)
            grad_query = (
                jnp.einsum("hqk,khd->qhd", grad_scores, keys, preferred_element_type=single) * scale
            )
            grad_keys = (
                carry[0]
                + jnp.einsum(
                    "hqk,qhd->khd", grad_scores, query_block, preferred_element_type=single
                )
                * scale
            )
            grad_values = carry[1] + jnp.einsum(
                "hqk,qhd->khd", probs.astype(half), grad_block, preferred_element_type=single
            )
            return ((grad_keys, grad_values), grad_query.astype(half))

        empty = jnp.zeros((seq_len, local_heads, head_dim), single)
        (grad_keys, grad_values), grad_queries = lax.scan(
            one_block, (empty, empty), (query_blocks, grad_blocks, sums)
        )
        return (
            grad_queries.reshape(seq_len, 1, span),
            grad_keys.astype(half).reshape(seq_len, 1, span),
            grad_values.astype(half).reshape(seq_len, 1, span),
        )

    grad_query_h, grad_keyed_h, grad_valued_h = lax.map(
        attend_back, (query_h, keyed_h, valued_h, grad_context_h, logsum, key_valid)
    )
    grad_query, grad_keyed, grad_valued = (
        lax.all_to_all(grad_query_h, "seq", split_axis=1, concat_axis=2, tiled=True),
        lax.all_to_all(grad_keyed_h, "seq", split_axis=1, concat_axis=2, tiled=True),
        lax.all_to_all(grad_valued_h, "seq", split_axis=1, concat_axis=2, tiled=True),
    )
    grad_query = grad_query.reshape(rows, width)
    grad_keyed = grad_keyed.reshape(rows, width)
    grad_valued = grad_valued.reshape(rows, width)
    grad_qkv = jnp.concatenate([grad_query, grad_keyed, grad_valued], axis=1)
    grad_wqkv = jnp.dot(hidden1.T, grad_qkv, preferred_element_type=single)
    grad_qbias = jnp.sum(grad_query.astype(single), axis=0)
    grad_vbias = jnp.sum(grad_valued.astype(single), axis=0)
    grad_hidden1 = jnp.dot(grad_qkv, wqkv_b.T, preferred_element_type=single)
    grad_state_norm, grad_gain1, grad_bias1 = norm1_back(grad_hidden1)
    grad_in = (grad_middle + grad_state_norm).reshape(clips, frames, width)
    gradients = (
        grad_gain1,
        grad_bias1,
        grad_wqkv,
        grad_qbias,
        grad_vbias,
        grad_wout,
        grad_obias,
        grad_gain2,
        grad_bias2,
        grad_wup,
        grad_ubias,
        grad_wdown,
        grad_dbias,
    )
    owned = (
        lax.psum_scatter(
            gradients[0].astype(jnp.bfloat16), "fsdp", scatter_dimension=0, tiled=True
        ).astype(jnp.float32),
        lax.psum_scatter(
            gradients[1].astype(jnp.bfloat16), "fsdp", scatter_dimension=0, tiled=True
        ).astype(jnp.float32),
        lax.psum_scatter(
            gradients[2].astype(jnp.bfloat16), "fsdp", scatter_dimension=0, tiled=True
        ).astype(jnp.float32),
        lax.psum_scatter(
            gradients[3].astype(jnp.bfloat16), "fsdp", scatter_dimension=0, tiled=True
        ).astype(jnp.float32),
        lax.psum_scatter(
            gradients[4].astype(jnp.bfloat16), "fsdp", scatter_dimension=0, tiled=True
        ).astype(jnp.float32),
        lax.psum_scatter(
            gradients[5].astype(jnp.bfloat16), "fsdp", scatter_dimension=0, tiled=True
        ).astype(jnp.float32),
        lax.psum_scatter(
            gradients[6].astype(jnp.bfloat16), "fsdp", scatter_dimension=0, tiled=True
        ).astype(jnp.float32),
        lax.psum_scatter(
            gradients[7].astype(jnp.bfloat16), "fsdp", scatter_dimension=0, tiled=True
        ).astype(jnp.float32),
        lax.psum_scatter(
            gradients[8].astype(jnp.bfloat16), "fsdp", scatter_dimension=0, tiled=True
        ).astype(jnp.float32),
        lax.psum_scatter(
            gradients[9].astype(jnp.bfloat16), "fsdp", scatter_dimension=0, tiled=True
        ).astype(jnp.float32),
        lax.psum_scatter(
            gradients[10].astype(jnp.bfloat16), "fsdp", scatter_dimension=0, tiled=True
        ).astype(jnp.float32),
        lax.psum_scatter(
            gradients[11].astype(jnp.bfloat16), "fsdp", scatter_dimension=0, tiled=True
        ).astype(jnp.float32),
        lax.psum_scatter(
            gradients[12].astype(jnp.bfloat16), "fsdp", scatter_dimension=0, tiled=True
        ).astype(jnp.float32),
    )
    reduced = (
        lax.psum(owned[0].astype(jnp.bfloat16), "seq").astype(jnp.float32),
        lax.psum(owned[1].astype(jnp.bfloat16), "seq").astype(jnp.float32),
        lax.psum(owned[2].astype(jnp.bfloat16), "seq").astype(jnp.float32),
        lax.psum(owned[3].astype(jnp.bfloat16), "seq").astype(jnp.float32),
        lax.psum(owned[4].astype(jnp.bfloat16), "seq").astype(jnp.float32),
        lax.psum(owned[5].astype(jnp.bfloat16), "seq").astype(jnp.float32),
        lax.psum(owned[6].astype(jnp.bfloat16), "seq").astype(jnp.float32),
        lax.psum(owned[7].astype(jnp.bfloat16), "seq").astype(jnp.float32),
        lax.psum(owned[8].astype(jnp.bfloat16), "seq").astype(jnp.float32),
        lax.psum(owned[9].astype(jnp.bfloat16), "seq").astype(jnp.float32),
        lax.psum(owned[10].astype(jnp.bfloat16), "seq").astype(jnp.float32),
        lax.psum(owned[11].astype(jnp.bfloat16), "seq").astype(jnp.float32),
        lax.psum(owned[12].astype(jnp.bfloat16), "seq").astype(jnp.float32),
        lax.psum(part_loss.astype(jnp.bfloat16), "seq").astype(jnp.float32),
    )
    summed = tuple(reduced[:13])
    clip_loss = reduced[13]
    return (
        frames_out,
        clip_loss,
        grad_in,
        summed[0],
        summed[1],
        summed[2],
        summed[3],
        summed[4],
        summed[5],
        summed[6],
        summed[7],
        summed[8],
        summed[9],
        summed[10],
        summed[11],
        summed[12],
    )


def solution(mesh):
    placed = (
        P("fsdp", "seq", None),
        P("fsdp", "seq", None),
        P(),
        P("fsdp"),
        P("fsdp"),
        P("fsdp", None),
        P("fsdp"),
        P("fsdp"),
        P("fsdp", None),
        P("fsdp"),
        P("fsdp"),
        P("fsdp"),
        P("fsdp", None),
        P("fsdp"),
        P("fsdp", None),
        P("fsdp"),
    )
    return jax.shard_map(
        local,
        mesh=mesh,
        in_specs=placed,
        out_specs=(
            P("fsdp", "seq", None),
            P("fsdp"),
            P("fsdp", "seq", None),
            P("fsdp"),
            P("fsdp"),
            P("fsdp", None),
            P("fsdp"),
            P("fsdp"),
            P("fsdp", None),
            P("fsdp"),
            P("fsdp"),
            P("fsdp"),
            P("fsdp", None),
            P("fsdp"),
            P("fsdp", None),
            P("fsdp"),
        ),
        check_vma=False,
    )
```

profile of v0, /device:TPU:0, one launch (start us, length us, event | category | flops | bytes accessed | tf_op | source)
XLA Modules:
  0.0 1777.0 jit_solution(1138143871130389060)
XLA Ops:
  18.2 41.9 %all-reduce.18 = (bf16[1280]{0:T(1024)(128)(2,1)S(1)}, bf16[1280]{0:T(1024)(128)(2,1)S(1)}, bf16[1280]{0:T(1024)(128)(2,1)S(1)}, bf16[1280]{0:T(1024)(128)(2,1)S...) all-reduce(bf16[1280]{0:T(1024)(128)(2,1)S(1)} %dynamic-update-slic, ...), channel_id=1, replica_groups=mesh['fsdp'=8,'seq'=4] {'fsdp'}, use_global_device_ids=true, to_apply=%add.1 | all-reduce | flops 10240 | bytes 40960
  63.8 92.2 %all-gather.6.cloned.1.call-done = bf16[1280,3840]{1,0:T(8,128)(2,1)} async-done(((bf16[160,3840]{1,0:T(8,128)(2,1)}), bf16[1280,3840]{1,0:T(8,128)(2,1)}) %all-gather.6.cloned.1.call-update) | async-done | bytes 9830416 | tf_op jit(solution)/shard_map/all_gather | solution.py:41
  194.7 15.3 all-to-all-done
  273.6 70.0 %while.54 = (s32[]{:T(128)}, bf16[2,1536,320]{1,2,0:T(8,128)(2,1)}, f32[2,3,4,512]{3,2,1,0:T(4,128)S(1)}, bf16[2,1536,4,80]{1,3,2,0:T(8,128)(2,1)}, bf16[2,1536,...) while((s32[]{:T(128)}, bf16[2,1536,320]{1,2,0:T(8,128)(2,1)}, ...), condition=%wide.region_7.8_spmd, body=%wide.region_2.7_spmd.sunk | while | flops 1044543488 | bytes 64087352 | solution.py:109
  277.6 27.9 %while.57 = (s32[]{:T(128)}, bf16[3,512,4,80]{1,3,2,0:T(8,128)(2,1)S(1)}, f32[3,4,512]{2,1,0:T(4,128)S(1)}, pred[1536]{0:T(1024)(128)(4,1)S(1)}, bf16[3,512,4,80...) while((s32[]{:T(128)}, ...), condition=%wide.region_6.6_spmd, body=%wide.region_3.5_spmd.sunk | while | flops 1044543488 | bytes 40441440 | solution.py:106
  312.5 27.8 %while.57 = (s32[]{:T(128)}, bf16[3,512,4,80]{1,3,2,0:T(8,128)(2,1)S(1)}, f32[3,4,512]{2,1,0:T(4,128)S(1)}, pred[1536]{0:T(1024)(128)(4,1)S(1)}, bf16[3,512,4,80...) while((s32[]{:T(128)}, ...), condition=%wide.region_6.6_spmd, body=%wide.region_3.5_spmd.sunk | while | flops 1044543488 | bytes 40441440 | solution.py:106
  354.8 31.4 %all-gather = bf16[8,1,640]{2,1,0:T(2,128)(2,1)S(1)} all-gather(bf16[1,1,640]{2,1,0:T(2,128)(2,1)S(1)} %reshape.315), channel_id=1, replica_groups=mesh['fsdp'=8,'seq'=4] {'fsdp'}, dimensions={0}, use_global_device_ids=true | all-gather | bytes 11520 | tf_op jit(solution)/shard_map/all_gather | solution.py:49
  408.8 51.7 %multiply_convert_fusion.1 = (bf16[768,5120]{1,0:T(8,128)(2,1)}, f32[768,5120]{1,0:T(8,128)}, f32[768,5120]{1,0:T(8,128)}) fusion(f32[5120]{0:T(1024)S(1)} %bitcast.260, bf16[1280,5120]{1,0:T(8,128)(2,1)} %all-gather.10.cloned.1.call-done, f32[768,1280]{1,0:T(8,128)} %copy-done.6, f32[1280]{0:T(1024)S(1)} %convert_element_type.214, ...), kind=kOutput, calls=%fused_computation.64 | convolution fusion | flops 10330767360 | bytes 56397824 | tf_op jit(solution)/shard_map/dot_general | solution.py:117
  460.5 123.9 %all-gather.12.cloned.1.call-done = bf16[5120,1280]{1,0:T(8,128)(2,1)} async-done(((bf16[640,1280]{1,0:T(8,128)(2,1)}), bf16[5120,1280]{1,0:T(8,128)(2,1)}) %all-gather.12.cloned.1.call-update) | async-done | bytes 13107216 | tf_op jit(solution)/shard_map/all_gather | solution.py:50
  584.3 18.9 %fusion.45 = (f32[768]{0:T(1024)}, bf16[768,1280]{1,0:T(8,128)(2,1)}, f32[768,1280]{1,0:T(8,128)S(1)}) fusion(f32[768]{0:T(1024)S(1)} %compare_convert_fusion, bf16[2,384,1280]{2,1,0:T(8,128)(2,1)S(1)} %copy-done.16, f32[1280]{0:T(1024)S(1)} %convert_element_type.218, f32[768,1280]{1,0:T(8,128)} %copy-done.6, bf16[768,5120]{1,0:T(8,128)(2,1)} %get-tuple-element.481, ...), kind=kOutput, calls=%fused_computation.86 | convolution fusion | flops 10074192896 | bytes 32779264 | tf_op jit(solution)/shard_map/dot_general | solution.py:120
  606.3 24.6 %fusion.68 = (bf16[5120]{0:T(1024)(128)(2,1)}, bf16[768,5120]{1,0:T(8,128)(2,1)}) fusion(f32[768,5120]{1,0:T(8,128)} %get-tuple-element.482, f32[768,5120]{1,0:T(8,128)} %get-tuple-element.501, f32[5120]{0:T(1024)S(1)} %bitcast.261, bf16[768,1280]{1,0:T(8,128)(2,1)} %get-tuple-element.474, bf16[5120,1280]{1,0:T(8,128)(2,1)} %all-gather.12.cloned.1.call-done), kind=kOutput, calls=%fused_computation.142 | convolution fusion | flops 10129239040 | bytes 54425600 | tf_op jit(solution)/shard_map/dot_general | solution.py:136
  630.9 19.5 %multiply_reduce_fusion.1 = (bf16[1280]{0:T(1024)(128)(2,1)}, f32[768]{0:T(1024)S(1)}, bf16[1280]{0:T(1024)(128)(2,1)}, f32[768,1280]{1,0:T(8,128)}) fusion(f32[768,1280]{1,0:T(8,128)} %copy-done.6, f32[768]{0:T(1024)S(1)} %fusion.60, f32[768]{0:T(1024)S(1)} %broadcast_multiply_fusion, f32[1280]{0:T(1024)S(1)} %convert_element_type.213, ...), kind=kOutput, calls=%fused_computation.108 | convolution fusion | flops 10074190848 | bytes 28855296 | tf_op jit(solution)/shard_map/dot_general | solution.py:141
  674.4 24.2 %all-to-all-done.4 = bf16[2,384,4,320]{1,0,3,2:T(2,128)(2,1)S(1)} async-done(((bf16[2,384,4,320]{1,0,3,2:T(2,128)(2,1)}), bf16[2,384,4,320]{1,0,3,2:T(2,128)(2,1)S(1)}, u32[]{:S(2)}, u32[]{:S(2)}) %all-to-all-start.4) | async-done | bytes 1966112 | tf_op jit(solution)/shard_map/all_to_all | solution.py:148
  705.6 227.1 %while.56 = (s32[]{:T(128)}, bf16[2,1536,1,320]{1,3,2,0:T(8,128)(2,1)}, bf16[2,1536,1,320]{1,3,2,0:T(8,128)(2,1)}, bf16[2,1536,1,320]{1,3,2,0:T(8,128)(2,1)}, bf...) while((s32[]{:T(128)}, ...), condition=%wide.region_20.21_spmd, body=%wide.region_16.20_spmd.sunk | while | flops 2548660224 | bytes 254784048 | solution.py:196
  714.5 93.9 %while.58 = (s32[]{:T(128)}, f32[1536,4,80]{0,2,1:T(8,128)S(1)}, f32[1536,4,80]{0,2,1:T(8,128)}, bf16[3,512,4,80]{1,3,2,0:T(8,128)(2,1)}, bf16[3,512,4,80]{1,3,2...) while((s32[]{:T(128)}, f32[1536,4,80]{0,2,1:T(8,128)S(1)}, ...), condition=%wide.region_19.19_spmd.clone, body=%wide.region_17.18_spmd.clone.sunk | while | flops 2547677184 | bytes 207532240 | solution.py:187
  828.0 93.9 %while.58 = (s32[]{:T(128)}, f32[1536,4,80]{0,2,1:T(8,128)S(1)}, f32[1536,4,80]{0,2,1:T(8,128)}, bf16[3,512,4,80]{1,3,2,0:T(8,128)(2,1)}, bf16[3,512,4,80]{1,3,2...) while((s32[]{:T(128)}, f32[1536,4,80]{0,2,1:T(8,128)S(1)}, ...), condition=%wide.region_19.19_spmd.clone, body=%wide.region_17.18_spmd.clone.sunk | while | flops 2547677184 | bytes 207532240 | solution.py:187
  982.8 21.7 %all-to-all-done.6 = bf16[2,1536,1,320]{3,0,2,1:T(2,128)(2,1)} async-done(((bf16[2,1536,1,320]{3,0,2,1:T(2,128)(2,1)}), bf16[2,1536,1,320]{3,0,2,1:T(2,128)(2,1)}, u32[]{:S(2)}, u32[]{:S(2)}) %all-to-all-start.6) | async-done | bytes 1966112 | tf_op jit(solution)/shard_map/all_to_all | solution.py:201
  1061.5 17.3 convolution_convert_fusion.1
  1080.3 16.3 convolution_convert_fusion
  1113.5 114.4 %reduce-scatter.5.cloned.1.call-done = bf16[160,3840]{1,0:T(8,128)(2,1)} async-done(((bf16[1280,3840]{1,0:T(8,128)(2,1)}), bf16[160,3840]{1,0:T(8,128)(2,1)}) %reduce-scatter.5.cloned.1.call-update) | async-done | bytes 1228816 | tf_op jit(solution)/shard_map/reduce_scatter | solution.py:236
  1227.9 217.4 %reduce-scatter.9.cloned.1.call-done = bf16[160,5120]{1,0:T(8,128)(2,1)} async-done(((bf16[1280,5120]{1,0:T(8,128)(2,1)}), bf16[160,5120]{1,0:T(8,128)(2,1)}) %reduce-scatter.9.cloned.1.call-update) | async-done | bytes 1638416 | tf_op jit(solution)/shard_map/reduce_scatter | solution.py:257
  1445.3 217.5 %reduce-scatter.11.cloned.1.call-done = bf16[640,1280]{1,0:T(8,128)(2,1)} async-done(((bf16[5120,1280]{1,0:T(8,128)(2,1)}), bf16[640,1280]{1,0:T(8,128)(2,1)}) %reduce-scatter.11.cloned.1.call-update) | async-done | bytes 1638416 | tf_op jit(solution)/shard_map/reduce_scatter | solution.py:263
  1671.7 35.7 %all-reduce.17 = (bf16[1280]{0:T(1024)(128)(2,1)S(1)}, bf16[1280]{0:T(1024)(128)(2,1)S(1)}, bf16[1280]{0:T(1024)(128)(2,1)S(1)}, bf16[1280]{0:T(1024)(128)(2,1)S...) all-reduce(bf16[1280]{0:T(1024)(128)(2,1)S(1)} %get-tuple-element.3, ...), channel_id=2, replica_groups=mesh['fsdp'=8,'seq'=4] {'fsdp'}, use_global_device_ids=true, to_apply=%region_24.25.clone | all-reduce | flops 15360 | bytes 61440
  1725.6 36.5 %all-reduce.23.cloned.1.call-done = (bf16[160,3840]{1,0:T(8,128)(2,1)}, bf16[160,1280]{1,0:T(8,128)(2,1)}, bf16[160,5120]{1,0:T(8,128)(2,1)}, bf16[640,1280]{1,0:T(8,128)(2,1)}) async-done(((bf16[160,3840]{1,0:T(8,128)(2,1)}, bf16[160,1280]{1,0:T(8,128)(2,1)}, bf16[160,5120]{1,0:T(8,128)(2,1)}, bf16[640,1280]{1,0:T(8,128)(2,1)}), (bf16[160,3840]{1,0:T(8,128)(2,1)}, bf16[160,1280]{1,0:T(8,128)(2,1)}, ...) | async-done | bytes 4915216 | tf_op jit(solution)/shard_map/psum | solution.py:273
  (454 shorter events, 638.0 us)
Async XLA Ops:
  7.2 148.8 %all-gather.6.cloned.1.call-start = ((), (), s32[]{:S(2)}) async-start(), calls=%async_computation.12 | async-start | bytes 11059200 | tf_op jit(solution)/shard_map/all_gather | solution.py:41
  7.9 392.6 %all-gather.8.cloned.1.call-start = ((), (), s32[]{:S(2)}) async-start(), calls=%async_computation.13 | async-start | bytes 3686400 | tf_op jit(solution)/shard_map/all_gather | solution.py:44
  8.7 400.1 %all-gather.10.cloned.1.call-start = ((), (), s32[]{:S(2)}) async-start(), calls=%async_computation.14 | async-start | bytes 14745600 | tf_op jit(solution)/shard_map/all_gather | solution.py:48
  60.5 106.3 %copy-start.35 = (f32[768]{0:T(1024)}, f32[768]{0:T(1024)S(1)}, u32[]{:S(2)}) copy-start(f32[768]{0:T(1024)S(1)} %div.56) | copy-start | bytes 9220
  61.1 105.6 %copy-start.41 = (f32[768]{0:T(1024)}, f32[768]{0:T(1024)S(1)}, u32[]{:S(2)}) copy-start(f32[768]{0:T(1024)S(1)} %add.192) | copy-start | bytes 9220
  181.2 28.7 %all-to-all-start = ((bf16[2,384,4,320]{1,0,3,2:T(2,128)(2,1)}), bf16[2,384,4,320]{1,0,3,2:T(2,128)(2,1)}, u32[]{:S(2)}, u32[]{:S(2)}) async-start(bf16[2,384,4,320]{1,0,3,2:T(2,128)(2,1)} %copy.196), calls=%async_computation | async-start | bytes 3932160 | tf_op jit(solution)/shard_map/all_to_all | solution.py:79
  209.9 28.7 %all-to-all-start.2 = ((bf16[2,384,4,320]{1,0,3,2:T(2,128)(2,1)}), bf16[2,384,4,320]{1,0,3,2:T(2,128)(2,1)}, u32[]{:S(2)}, u32[]{:S(2)}) async-start(bf16[2,384,4,320]{1,0,3,2:T(2,128)(2,1)} %copy.198), calls=%async_computation.2 | async-start | bytes 3932160 | tf_op jit(solution)/shard_map/all_to_all | solution.py:81
  238.7 27.8 %all-to-all-start.1 = ((bf16[2,384,4,320]{1,0,3,2:T(2,128)(2,1)}), bf16[2,384,4,320]{1,0,3,2:T(2,128)(2,1)S(1)}, u32[]{:S(2)}, u32[]{:S(2)}) async-start(bf16[2,384,4,320]{1,0,3,2:T(2,128)(2,1)} %copy.197), calls=%async_computation.1 | async-start | bytes 3932160 | tf_op jit(solution)/shard_map/all_to_all | solution.py:80
  242.3 342.0 %all-gather.12.cloned.1.call-start = ((), (), s32[]{:S(2)}) async-start(), calls=%async_computation.15 | async-start | bytes 14745600 | tf_op jit(solution)/shard_map/all_gather | solution.py:50
  350.4 36.7 %all-to-all-start.3 = ((bf16[2,1536,1,320]{3,0,2,1:T(2,128)(2,1)}), bf16[2,1536,1,320]{3,0,2,1:T(2,128)(2,1)S(1)}, u32[]{:S(2)}, u32[]{:S(2)}) async-start(bf16[2,1536,1,320]{3,0,2,1:T(2,128)(2,1)} %bitcast.245), calls=%async_computation.3 | async-start | bytes 4718592 | tf_op jit(solution)/shard_map/all_to_all | solution.py:110
  354.7 295.7 %copy-start.45 = (f32[1280]{0:T(1024)}, f32[1280]{0:T(1024)S(1)}, u32[]{:S(2)}) copy-start(f32[1280]{0:T(1024)S(1)} %convert_element_type.213) | copy-start | bytes 15364
  354.8 54.0 %copy-start.52 = (f32[1280]{0:T(1024)}, f32[1280]{0:T(1024)S(1)}, u32[]{:S(2)}) copy-start(f32[1280]{0:T(1024)S(1)} %convert_element_type.214) | copy-start | bytes 15364
  406.2 244.2 %copy-start.39 = (f32[768]{0:T(1024)}, f32[768]{0:T(1024)S(1)}, u32[]{:S(2)}) copy-start(f32[768]{0:T(1024)S(1)} %broadcast_multiply_fusion) | copy-start | bytes 9220
  408.7 241.7 %copy-start.47 = (f32[768]{0:T(1024)}, f32[768]{0:T(1024)S(1)}, u32[]{:S(2)}) copy-start(f32[768]{0:T(1024)S(1)} %fusion.60) | copy-start | bytes 9220
  408.7 175.6 %copy-start.16 = (bf16[2,384,1280]{2,1,0:T(8,128)(2,1)S(1)}, bf16[2,384,1280]{2,1,0:T(8,128)(2,1)}, u32[]{:S(2)}) copy-start(bf16[2,384,1280]{2,1,0:T(8,128)(2,1)} %param.25) | copy-start | bytes 5898244
  670.7 27.8 %all-to-all-start.4 = ((bf16[2,384,4,320]{1,0,3,2:T(2,128)(2,1)}), bf16[2,384,4,320]{1,0,3,2:T(2,128)(2,1)S(1)}, u32[]{:S(2)}, u32[]{:S(2)}) async-start(bf16[2,384,4,320]{1,0,3,2:T(2,128)(2,1)} %copy.199), calls=%async_computation.4 | async-start | bytes 3932160 | tf_op jit(solution)/shard_map/all_to_all | solution.py:148
  939.4 32.1 %all-to-all-start.5 = ((bf16[2,1536,1,320]{3,0,2,1:T(2,128)(2,1)}), bf16[2,1536,1,320]{3,0,2,1:T(2,128)(2,1)S(1)}, u32[]{:S(2)}, u32[]{:S(2)}) async-start(bf16[2,1536,1,320]{3,0,2,1:T(2,128)(2,1)} %copy.185), calls=%async_computation.5 | async-start | bytes 4718592 | tf_op jit(solution)/shard_map/all_to_all | solution.py:200
  943.1 170.4 %reduce-scatter.7.cloned.1.call-start = ((), (), s32[]{:S(2)}) async-start(), calls=%async_computation.17 | async-start | bytes 3686400 | tf_op jit(solution)/shard_map/reduce_scatter | solution.py:245
  971.5 33.0 %all-to-all-start.6 = ((bf16[2,1536,1,320]{3,0,2,1:T(2,128)(2,1)}), bf16[2,1536,1,320]{3,0,2,1:T(2,128)(2,1)}, u32[]{:S(2)}, u32[]{:S(2)}) async-start(bf16[2,1536,1,320]{3,0,2,1:T(2,128)(2,1)} %copy.188), calls=%async_computation.6 | async-start | bytes 4718592 | tf_op jit(solution)/shard_map/all_to_all | solution.py:201
  1004.6 33.1 %all-to-all-start.7 = ((bf16[2,1536,1,320]{3,0,2,1:T(2,128)(2,1)}), bf16[2,1536,1,320]{3,0,2,1:T(2,128)(2,1)}, u32[]{:S(2)}, u32[]{:S(2)}) async-start(bf16[2,1536,1,320]{3,0,2,1:T(2,128)(2,1)} %copy.191), calls=%async_computation.7 | async-start | bytes 4718592 | tf_op jit(solution)/shard_map/all_to_all | solution.py:202
  1009.1 218.8 %reduce-scatter.5.cloned.1.call-start = ((), (), s32[]{:S(2)}) async-start(), calls=%async_computation.16 | async-start | bytes 11059200 | tf_op jit(solution)/shard_map/reduce_scatter | solution.py:236
  1060.8 384.5 %reduce-scatter.9.cloned.1.call-start = ((), (), s32[]{:S(2)}) async-start(), calls=%async_computation.18 | async-start | bytes 14745600 | tf_op jit(solution)/shard_map/reduce_scatter | solution.py:257
  1078.8 584.0 %reduce-scatter.11.cloned.1.call-start = ((), (), s32[]{:S(2)}) async-start(), calls=%async_computation.19 | async-start | bytes 14745600 | tf_op jit(solution)/shard_map/reduce_scatter | solution.py:263
  1096.7 665.4 %all-reduce.23.cloned.1.call-start = ((), (), s32[]{:S(2)}) async-start(), calls=%async_computation.20 | async-start | bytes 9830400 | tf_op jit(solution)/shard_map/psum | solution.py:273
  (73 other events, 582.0 us)
Sparse Core Ops, SparseCore 0:
  10.2 145.8 all-gather.5
  158.2 59.6 all-gather.7
  220.1 181.2 all-gather.9
  403.4 180.8 all-gather.11
  950.4 74.5 reduce-scatter.6
  1060.9 166.9 reduce-scatter.4
  1231.5 213.7 reduce-scatter.8
  1449.0 213.8 reduce-scatter.10
  1665.4 96.6 all-reduce.22
where the time goes:
time: 1790 us; the launch traced here: 1780 us
  waiting for transfers between devices  905 us (51%)
  matrix products  379 us (21%)
  local copies, waits for them, and re-layouts  240 us (13%)
  blocking collectives  115 us (6%)
  other arithmetic  85 us (5%)
  starting transfers between devices  34 us (2%)
    reduce_scatter x1, waiting for transfers between devices, local(): lax.psum_scatter(gradients[11].astype(jnp.bfloat16), 'fsdp', scatter_dime...  217 us
    reduce_scatter x1, waiting for transfers between devices, local(): lax.psum_scatter(gradients[9].astype(jnp.bfloat16), 'fsdp', scatter_dimen...  217 us
    all_gather x1, waiting for transfers between devices, local(): lax.all_gather(w_down, 'fsdp', axis=0, tiled=True)  124 us
    reduce_scatter x1, waiting for transfers between devices, local(): lax.psum_scatter(gradients[2].astype(jnp.bfloat16), 'fsdp', scatter_dimen...  114 us
    all_gather x1, waiting for transfers between devices, local(): lax.all_gather(w_qkv, 'fsdp', axis=0, tiled=True)  92.2 us
    unnamed x2, blocking collectives  77.6 us
    dot_general x1, matrix products, local(): jnp.dot(hidden2, wup, preferred_element_type=single) + ubias.astype(single)  51.7 us
    dot_general x12, matrix products, scores_of(): jnp.einsum('qhd,khd->hqk', query_block, keys, preferred_element_type=single)  45.4 us
  transfers between devices with their start and end apart: 17, of which 13 were waited for; matrix products, arithmetic and copies ran while one was open for 20% of the time, Pallas kernels for 0%

commit v1 on v0

--- a/solution.py
+++ b/solution.py
@@ -33,6 +33,10 @@
     w_down,
     down_bias,
 ):
+
+    def _compute_seats_all(field_in):
+        return lax.all_gather(field_in, "seq").sum(axis=0)
+
     single = jnp.float32
     half = jnp.bfloat16
     gain1, bias1, wqkv, qbias, vbias, wout, obias, gain2, bias2, wup, ubias, wdown, dbias = (
@@ -270,7 +274,7 @@
     reduced = (
         lax.psum(owned[0].astype(jnp.bfloat16), "seq").astype(jnp.float32),
         lax.psum(owned[1].astype(jnp.bfloat16), "seq").astype(jnp.float32),
-        lax.psum(owned[2].astype(jnp.bfloat16), "seq").astype(jnp.float32),
+        _compute_seats_all(owned[2].astype(jnp.bfloat16)).astype(jnp.float32),
         lax.psum(owned[3].astype(jnp.bfloat16), "seq").astype(jnp.float32),
         lax.psum(owned[4].astype(jnp.bfloat16), "seq").astype(jnp.float32),
         lax.psum(owned[5].astype(jnp.bfloat16), "seq").astype(jnp.float32),

time: 1790 us -> 1490 us (0.83)
  waiting for transfers between devices: 905 us -> 599 us
    reduce_scatter x1, waiting for transfers between devices: 217 us -> 0.02 us  [local(): lax.psum_scatter(gradients[9].astype(jnp.bfloat16), 'fsdp', scatter_dimen...]
    reduce_scatter x1, waiting for transfers between devices: 217 us -> 82.2 us  [local(): lax.psum_scatter(gradients[11].astype(jnp.bfloat16), 'fsdp', scatter_dime...]
    reduce_scatter x1, waiting for transfers between devices: 114 us -> 172 us  [local(): lax.psum_scatter(gradients[2].astype(jnp.bfloat16), 'fsdp', scatter_dimen...]
    psum x1, waiting for transfers between devices: 36.5 us -> 0.37 us  [local(): lax.psum(owned[5].astype(jnp.bfloat16), 'seq').astype(jnp.float32)]
    all_gather x0 -> x1, waiting for transfers between devices: none -> 33.5 us  [_compute_seats_all(): return lax.all_gather(field_in, 'seq').sum(axis=0)]
  transfers between devices with their start and end apart: 17 -> 18, of which waited for: 13 -> 13; matrix products, arithmetic and copies ran while one was open for 20% -> 39% of each run, Pallas kernels for 0% -> 0%
where the time goes in v1:
time: 1490 us; the launch traced here: 1480 us
  waiting for transfers between devices  599 us (40%)
  matrix products  378 us (25%)
  local copies, waits for them, and re-layouts  244 us (16%)
  blocking collectives  116 us (8%)
  other arithmetic  85.6 us (6%)
  starting transfers between devices  33.4 us (2%)
  between operations  18 us (1%)
    reduce_scatter x1, waiting for transfers between devices, local(): lax.psum_scatter(gradients[2].astype(jnp.bfloat16), 'fsdp', scatter_dimen...  172 us
    all_gather x1, waiting for transfers between devices, local(): lax.all_gather(w_down, 'fsdp', axis=0, tiled=True)  124 us
    all_gather x1, waiting for transfers between devices, local(): lax.all_gather(w_qkv, 'fsdp', axis=0, tiled=True)  92.2 us
    reduce_scatter x1, waiting for transfers between devices, local(): lax.psum_scatter(gradients[11].astype(jnp.bfloat16), 'fsdp', scatter_dime...  82.2 us
    unnamed x2, blocking collectives  78 us
    dot_general x1, matrix products, local(): jnp.dot(hidden2, wup, preferred_element_type=single) + ubias.astype(single)  51.6 us
    dot_general x12, matrix products, scores_of(): jnp.einsum('qhd,khd->hqk', query_block, keys, preferred_element_type=single)  45.4 us
    dot_general x6, matrix products, one_block(): jnp.einsum('hqk,khd->qhd', grad_scores, keys, preferred_element_type=single)  39.5 us
  transfers between devices with their start and end apart: 18, of which 13 were waited for; matrix products, arithmetic and copies ran while one was open for 39% of the time, Pallas kernels for 0%

profile of v1, /device:TPU:0, one launch (start us, length us, event | category | flops | bytes accessed | tf_op | source)
XLA Modules:
  0.0 1475.1 jit_solution(9564663880637217557)
XLA Ops:
  18.2 41.9 %all-reduce.18 = (bf16[1280]{0:T(1024)(128)(2,1)S(1)}, bf16[1280]{0:T(1024)(128)(2,1)S(1)}, bf16[1280]{0:T(1024)(128)(2,1)S(1)}, bf16[1280]{0:T(1024)(128)(2,1)S...) all-reduce(bf16[1280]{0:T(1024)(128)(2,1)S(1)} %dynamic-update-slic, ...), channel_id=1, replica_groups=mesh['fsdp'=8,'seq'=4] {'fsdp'}, use_global_device_ids=true, to_apply=%add.1 | all-reduce | flops 10240 | bytes 40960
  63.9 92.2 %all-gather.8.cloned.1.call-done = bf16[1280,3840]{1,0:T(8,128)(2,1)} async-done(((bf16[160,3840]{1,0:T(8,128)(2,1)}), bf16[1280,3840]{1,0:T(8,128)(2,1)}) %all-gather.8.cloned.1.call-update) | async-done | bytes 9830416 | tf_op jit(solution)/shard_map/all_gather | solution.py:45
  194.8 15.3 %all-to-all-done = bf16[2,384,4,320]{1,0,3,2:T(2,128)(2,1)} async-done(((bf16[2,384,4,320]{1,0,3,2:T(2,128)(2,1)}), bf16[2,384,4,320]{1,0,3,2:T(2,128)(2,1)}, u32[]{:S(2)}, u32[]{:S(2)}) %all-to-all-start) | async-done | bytes 1966112 | tf_op jit(solution)/shard_map/all_to_all | solution.py:83
  273.7 70.0 %while.54 = (s32[]{:T(128)}, bf16[2,1536,320]{1,2,0:T(8,128)(2,1)}, f32[2,3,4,512]{3,2,1,0:T(4,128)S(1)}, bf16[2,1536,4,80]{1,3,2,0:T(8,128)(2,1)}, bf16[2,1536,...) while((s32[]{:T(128)}, bf16[2,1536,320]{1,2,0:T(8,128)(2,1)}, ...), condition=%wide.region_7.8_spmd, body=%wide.region_2.7_spmd.sunk | while | flops 1044543488 | bytes 64087352 | solution.py:113
  277.7 27.9 %while.57 = (s32[]{:T(128)}, bf16[3,512,4,80]{1,3,2,0:T(8,128)(2,1)S(1)}, f32[3,4,512]{2,1,0:T(4,128)S(1)}, pred[1536]{0:T(1024)(128)(4,1)S(1)}, bf16[3,512,4,80...) while((s32[]{:T(128)}, ...), condition=%wide.region_6.6_spmd, body=%wide.region_3.5_spmd.sunk | while | flops 1044543488 | bytes 40441440 | solution.py:110
  312.7 27.8 %while.57 = (s32[]{:T(128)}, bf16[3,512,4,80]{1,3,2,0:T(8,128)(2,1)S(1)}, f32[3,4,512]{2,1,0:T(4,128)S(1)}, pred[1536]{0:T(1024)(128)(4,1)S(1)}, bf16[3,512,4,80...) while((s32[]{:T(128)}, ...), condition=%wide.region_6.6_spmd, body=%wide.region_3.5_spmd.sunk | while | flops 1044543488 | bytes 40441440 | solution.py:110
  355.0 31.4 %all-gather.1 = bf16[8,1,640]{2,1,0:T(2,128)(2,1)S(1)} all-gather(bf16[1,1,640]{2,1,0:T(2,128)(2,1)S(1)} %reshape.316), channel_id=1, replica_groups=mesh['fsdp'=8,'seq'=4] {'fsdp'}, dimensions={0}, use_global_device_ids=true | all-gather | bytes 11520 | tf_op jit(solution)/shard_map/all_gather | solution.py:53
  408.9 51.6 %multiply_convert_fusion.1 = (bf16[768,5120]{1,0:T(8,128)(2,1)}, f32[768,5120]{1,0:T(8,128)}, f32[768,5120]{1,0:T(8,128)}) fusion(f32[5120]{0:T(1024)S(1)} %bitcast.262, bf16[1280,5120]{1,0:T(8,128)(2,1)} %all-gather.12.cloned.1.call-done, f32[768,1280]{1,0:T(8,128)} %copy-done.6, f32[1280]{0:T(1024)S(1)} %convert_element_type.216, ...), kind=kOutput, calls=%fused_computation.64 | convolution fusion | flops 10330767360 | bytes 56397824 | tf_op jit(solution)/shard_map/dot_general | solution.py:121
  460.5 123.8 %all-gather.14.cloned.1.call-done = bf16[5120,1280]{1,0:T(8,128)(2,1)} async-done(((bf16[640,1280]{1,0:T(8,128)(2,1)}), bf16[5120,1280]{1,0:T(8,128)(2,1)}) %all-gather.14.cloned.1.call-update) | async-done | bytes 13107216 | tf_op jit(solution)/shard_map/all_gather | solution.py:54
  584.3 18.8 %fusion.45 = (f32[768]{0:T(1024)}, bf16[768,1280]{1,0:T(8,128)(2,1)}, f32[768,1280]{1,0:T(8,128)S(1)}) fusion(f32[768]{0:T(1024)S(1)} %compare_convert_fusion, bf16[2,384,1280]{2,1,0:T(8,128)(2,1)S(1)} %copy-done.18, f32[1280]{0:T(1024)S(1)} %convert_element_type.220, f32[768,1280]{1,0:T(8,128)} %copy-done.6, bf16[768,5120]{1,0:T(8,128)(2,1)} %get-tuple-element.480, ...), kind=kOutput, calls=%fused_computation.86 | convolution fusion | flops 10074192896 | bytes 32779264 | tf_op jit(solution)/shard_map/dot_general | solution.py:124
  606.3 24.6 %fusion.68 = (bf16[5120]{0:T(1024)(128)(2,1)}, bf16[768,5120]{1,0:T(8,128)(2,1)}) fusion(f32[768,5120]{1,0:T(8,128)} %get-tuple-element.481, f32[768,5120]{1,0:T(8,128)} %get-tuple-element.500, f32[5120]{0:T(1024)S(1)} %bitcast.263, bf16[768,1280]{1,0:T(8,128)(2,1)} %get-tuple-element.473, bf16[5120,1280]{1,0:T(8,128)(2,1)} %all-gather.14.cloned.1.call-done), kind=kOutput, calls=%fused_computation.142 | convolution fusion | flops 10129239040 | bytes 54425600 | tf_op jit(solution)/shard_map/dot_general | solution.py:140
  630.9 19.5 %multiply_reduce_fusion.1 = (bf16[1280]{0:T(1024)(128)(2,1)}, f32[768]{0:T(1024)S(1)}, bf16[1280]{0:T(1024)(128)(2,1)}, f32[768,1280]{1,0:T(8,128)}) fusion(f32[768,1280]{1,0:T(8,128)} %copy-done.6, f32[768]{0:T(1024)S(1)} %fusion.60, f32[768]{0:T(1024)S(1)} %broadcast_multiply_fusion, f32[1280]{0:T(1024)S(1)} %convert_element_type.215, ...), kind=kOutput, calls=%fused_computation.108 | convolution fusion | flops 10074190848 | bytes 28855296 | tf_op jit(solution)/shard_map/dot_general | solution.py:145
  662.0 17.3 %convolution_convert_fusion.1 = bf16[1280,5120]{1,0:T(8,128)(2,1)} fusion(bf16[768,5120]{1,0:T(8,128)(2,1)} %get-tuple-element.475, f32[768,1280]{1,0:T(8,128)} %copy-done.6, f32[1280]{0:T(1024)S(1)} %convert_element_type.216, f32[1280]{0:T(1024)S(1)} %convert_element_type.215, f32[768]{0:T(1024)S(1)} %fusion.60, f32[768]{0:T(1024)S(1)} %broadcast_multiply_fusion), kind=kOutput, calls=%fused_computation.61 | convolution fusion | flops 10077798400 | bytes 24920064 | tf_op jit(solution)/shard_map/dot_general | solution.py:143
  700.1 16.4 %convolution_convert_fusion = bf16[5120,1280]{1,0:T(8,128)(2,1)} fusion(bf16[768,5120]{1,0:T(8,128)(2,1)} %get-tuple-element.480, bf16[768,1280]{1,0:T(8,128)(2,1)} %get-tuple-element.473), kind=kOutput, calls=%fused_computation.60 | convolution fusion | flops 10072883200 | bytes 22937600 | tf_op jit(solution)/shard_map/dot_general | solution.py:138
  731.3 229.4 %while.56 = (s32[]{:T(128)}, bf16[2,1536,1,320]{1,3,2,0:T(8,128)(2,1)}, bf16[2,1536,1,320]{1,3,2,0:T(8,128)(2,1)}, bf16[2,1536,1,320]{1,3,2,0:T(8,128)(2,1)}, bf...) while((s32[]{:T(128)}, ...), condition=%wide.region_20.21_spmd, body=%wide.region_16.20_spmd.sunk | while | flops 2548660224 | bytes 254784048 | solution.py:200
  740.6 94.6 %while.58 = (s32[]{:T(128)}, f32[1536,4,80]{0,2,1:T(8,128)S(1)}, f32[1536,4,80]{0,2,1:T(8,128)}, bf16[3,512,4,80]{1,3,2,0:T(8,128)(2,1)}, bf16[3,512,4,80]{1,3,2...) while((s32[]{:T(128)}, f32[1536,4,80]{0,2,1:T(8,128)S(1)}, ...), condition=%wide.region_19.19_spmd.clone, body=%wide.region_17.18_spmd.clone.sunk | while | flops 2547677184 | bytes 207532240 | solution.py:191
  855.0 95.0 %while.58 = (s32[]{:T(128)}, f32[1536,4,80]{0,2,1:T(8,128)S(1)}, f32[1536,4,80]{0,2,1:T(8,128)}, bf16[3,512,4,80]{1,3,2,0:T(8,128)(2,1)}, bf16[3,512,4,80]{1,3,2...) while((s32[]{:T(128)}, f32[1536,4,80]{0,2,1:T(8,128)S(1)}, ...), condition=%wide.region_19.19_spmd.clone, body=%wide.region_17.18_spmd.clone.sunk | while | flops 2547677184 | bytes 207532240 | solution.py:191
  977.9 21.7 %all-to-all-done.5 = bf16[2,1536,1,320]{3,0,2,1:T(2,128)(2,1)S(1)} async-done(((bf16[2,1536,1,320]{3,0,2,1:T(2,128)(2,1)}), bf16[2,1536,1,320]{3,0,2,1:T(2,128)(2,1)S(1)}, u32[]{:S(2)}, u32[]{:S(2)}) %all-to-all-start.5) | async-done | bytes 1966112 | tf_op jit(solution)/shard_map/all_to_all | solution.py:204
  1010.9 21.8 %all-to-all-done.6 = bf16[2,1536,1,320]{3,0,2,1:T(2,128)(2,1)} async-done(((bf16[2,1536,1,320]{3,0,2,1:T(2,128)(2,1)}), bf16[2,1536,1,320]{3,0,2,1:T(2,128)(2,1)}, u32[]{:S(2)}, u32[]{:S(2)}) %all-to-all-start.6) | async-done | bytes 1966112 | tf_op jit(solution)/shard_map/all_to_all | solution.py:205
  1089.1 82.2 %reduce-scatter.11.cloned.1.call-done = bf16[640,1280]{1,0:T(8,128)(2,1)} async-done(((bf16[5120,1280]{1,0:T(8,128)(2,1)}), bf16[640,1280]{1,0:T(8,128)(2,1)}) %reduce-scatter.11.cloned.1.call-update) | async-done | bytes 1638416 | tf_op jit(solution)/shard_map/reduce_scatter | solution.py:267
  1171.6 172.2 %reduce-scatter.5.cloned.1.call-done = bf16[160,3840]{1,0:T(8,128)(2,1)} async-done(((bf16[1280,3840]{1,0:T(8,128)(2,1)}), bf16[160,3840]{1,0:T(8,128)(2,1)}) %reduce-scatter.5.cloned.1.call-update) | async-done | bytes 1228816 | tf_op jit(solution)/shard_map/reduce_scatter | solution.py:240
  1350.6 13.7 fusion.65
  1368.3 36.1 %all-reduce.17 = (bf16[1280]{0:T(1024)(128)(2,1)S(1)}, bf16[1280]{0:T(1024)(128)(2,1)S(1)}, bf16[1280]{0:T(1024)(128)(2,1)S(1)}, bf16[1280]{0:T(1024)(128)(2,1)S...) all-reduce(bf16[1280]{0:T(1024)(128)(2,1)S(1)} %get-tuple-element.3, ...), channel_id=3, replica_groups=mesh['fsdp'=8,'seq'=4] {'fsdp'}, use_global_device_ids=true, to_apply=%region_24.25.clone | all-reduce | flops 15360 | bytes 61440
  1429.7 33.5 %all-gather.16.cloned.1.call-done = bf16[640,3840]{1,0:T(8,128)(2,1)} async-done(((bf16[160,3840]{1,0:T(8,128)(2,1)}), bf16[640,3840]{1,0:T(8,128)(2,1)}) %all-gather.16.cloned.1.call-update) | async-done | bytes 4915216 | tf_op jit(solution)/shard_map/all_gather | solution.py:38
  (442 shorter events, 621.8 us)
Async XLA Ops:
  7.2 148.8 %all-gather.8.cloned.1.call-start = ((), (), s32[]{:S(2)}) async-start(), calls=%async_computation.12 | async-start | bytes 11059200 | tf_op jit(solution)/shard_map/all_gather | solution.py:45
  7.9 392.8 %all-gather.10.cloned.1.call-start = ((), (), s32[]{:S(2)}) async-start(), calls=%async_computation.13 | async-start | bytes 3686400 | tf_op jit(solution)/shard_map/all_gather | solution.py:48
  8.7 400.2 %all-gather.12.cloned.1.call-start = ((), (), s32[]{:S(2)}) async-start(), calls=%async_computation.14 | async-start | bytes 14745600 | tf_op jit(solution)/shard_map/all_gather | solution.py:52
  60.5 106.4 %copy-start.35 = (f32[768]{0:T(1024)}, f32[768]{0:T(1024)S(1)}, u32[]{:S(2)}) copy-start(f32[768]{0:T(1024)S(1)} %div.56) | copy-start | bytes 9220
  181.3 28.8 %all-to-all-start = ((bf16[2,384,4,320]{1,0,3,2:T(2,128)(2,1)}), bf16[2,384,4,320]{1,0,3,2:T(2,128)(2,1)}, u32[]{:S(2)}, u32[]{:S(2)}) async-start(bf16[2,384,4,320]{1,0,3,2:T(2,128)(2,1)} %copy.196), calls=%async_computation | async-start | bytes 3932160 | tf_op jit(solution)/shard_map/all_to_all | solution.py:83
  210.0 28.8 %all-to-all-start.2 = ((bf16[2,384,4,320]{1,0,3,2:T(2,128)(2,1)}), bf16[2,384,4,320]{1,0,3,2:T(2,128)(2,1)}, u32[]{:S(2)}, u32[]{:S(2)}) async-start(bf16[2,384,4,320]{1,0,3,2:T(2,128)(2,1)} %copy.198), calls=%async_computation.2 | async-start | bytes 3932160 | tf_op jit(solution)/shard_map/all_to_all | solution.py:85
  238.8 27.8 %all-to-all-start.1 = ((bf16[2,384,4,320]{1,0,3,2:T(2,128)(2,1)}), bf16[2,384,4,320]{1,0,3,2:T(2,128)(2,1)S(1)}, u32[]{:S(2)}, u32[]{:S(2)}) async-start(bf16[2,384,4,320]{1,0,3,2:T(2,128)(2,1)} %copy.197), calls=%async_computation.1 | async-start | bytes 3932160 | tf_op jit(solution)/shard_map/all_to_all | solution.py:84
  242.4 341.9 %all-gather.14.cloned.1.call-start = ((), (), s32[]{:S(2)}) async-start(), calls=%async_computation.15 | async-start | bytes 14745600 | tf_op jit(solution)/shard_map/all_gather | solution.py:54
  350.6 36.7 %all-to-all-start.3 = ((bf16[2,1536,1,320]{3,0,2,1:T(2,128)(2,1)}), bf16[2,1536,1,320]{3,0,2,1:T(2,128)(2,1)S(1)}, u32[]{:S(2)}, u32[]{:S(2)}) async-start(bf16[2,1536,1,320]{3,0,2,1:T(2,128)(2,1)} %bitcast.246), calls=%async_computation.3 | async-start | bytes 4718592 | tf_op jit(solution)/shard_map/all_to_all | solution.py:114
  354.3 734.8 %reduce-scatter.7.cloned.1.call-start = ((), (), s32[]{:S(2)}) async-start(), calls=%async_computation.17 | async-start | bytes 3686400 | tf_op jit(solution)/shard_map/reduce_scatter | solution.py:249
  408.9 175.4 %copy-start.18 = (bf16[2,384,1280]{2,1,0:T(8,128)(2,1)S(1)}, bf16[2,384,1280]{2,1,0:T(8,128)(2,1)}, u32[]{:S(2)}) copy-start(bf16[2,384,1280]{2,1,0:T(8,128)(2,1)} %param.25) | copy-start | bytes 5898244
  662.0 427.1 %reduce-scatter.9.cloned.1.call-start = ((), (), s32[]{:S(2)}) async-start(), calls=%async_computation.18 | async-start | bytes 14745600 | tf_op jit(solution)/shard_map/reduce_scatter | solution.py:261
  696.4 27.8 %all-to-all-start.4 = ((bf16[2,384,4,320]{1,0,3,2:T(2,128)(2,1)}), bf16[2,384,4,320]{1,0,3,2:T(2,128)(2,1)S(1)}, u32[]{:S(2)}, u32[]{:S(2)}) async-start(bf16[2,384,4,320]{1,0,3,2:T(2,128)(2,1)} %copy.199), calls=%async_computation.4 | async-start | bytes 3932160 | tf_op jit(solution)/shard_map/all_to_all | solution.py:152
  700.0 471.3 %reduce-scatter.11.cloned.1.call-start = ((), (), s32[]{:S(2)}) async-start(), calls=%async_computation.19 | async-start | bytes 14745600 | tf_op jit(solution)/shard_map/reduce_scatter | solution.py:267
  967.5 32.1 %all-to-all-start.5 = ((bf16[2,1536,1,320]{3,0,2,1:T(2,128)(2,1)}), bf16[2,1536,1,320]{3,0,2,1:T(2,128)(2,1)S(1)}, u32[]{:S(2)}, u32[]{:S(2)}) async-start(bf16[2,1536,1,320]{3,0,2,1:T(2,128)(2,1)} %copy.185), calls=%async_computation.5 | async-start | bytes 4718592 | tf_op jit(solution)/shard_map/all_to_all | solution.py:204
  999.6 33.1 %all-to-all-start.6 = ((bf16[2,1536,1,320]{3,0,2,1:T(2,128)(2,1)}), bf16[2,1536,1,320]{3,0,2,1:T(2,128)(2,1)}, u32[]{:S(2)}, u32[]{:S(2)}) async-start(bf16[2,1536,1,320]{3,0,2,1:T(2,128)(2,1)} %copy.188), calls=%async_computation.6 | async-start | bytes 4718592 | tf_op jit(solution)/shard_map/all_to_all | solution.py:205
  1032.7 33.1 %all-to-all-start.7 = ((bf16[2,1536,1,320]{3,0,2,1:T(2,128)(2,1)}), bf16[2,1536,1,320]{3,0,2,1:T(2,128)(2,1)}, u32[]{:S(2)}, u32[]{:S(2)}) async-start(bf16[2,1536,1,320]{3,0,2,1:T(2,128)(2,1)} %copy.191), calls=%async_computation.7 | async-start | bytes 4718592 | tf_op jit(solution)/shard_map/all_to_all | solution.py:206
  1037.2 306.6 %reduce-scatter.5.cloned.1.call-start = ((), (), s32[]{:S(2)}) async-start(), calls=%async_computation.16 | async-start | bytes 11059200 | tf_op jit(solution)/shard_map/reduce_scatter | solution.py:240
  1089.0 256.1 %copy-start.50 = (f32[768]{0:T(1024)S(1)}, f32[768]{0:T(1024)}, u32[]{:S(2)}) copy-start(f32[768]{0:T(1024)} %get-tuple-element.494) | copy-start | bytes 9220
  1089.0 334.1 %all-reduce.23.cloned.1.call-start = ((), (), s32[]{:S(2)}) async-start(), calls=%async_computation.21 | async-start | bytes 7372800 | tf_op jit(solution)/shard_map/psum | solution.py:280
  1171.4 179.2 %copy-start.4 = (bf16[2,384,1280]{2,1,0:T(8,128)(2,1)S(1)}, bf16[2,384,1280]{2,1,0:T(8,128)(2,1)}, u32[]{:S(2)}) copy-start(bf16[2,384,1280]{2,1,0:T(8,128)(2,1)} %param.24) | copy-start | bytes 5898244
  1171.4 179.2 %copy-start.34 = (f32[1280]{0:T(1024)S(1)}, f32[1280]{0:T(1024)}, u32[]{:S(2)}) copy-start(f32[1280]{0:T(1024)} %copy-done.33) | copy-start | bytes 15364
  1171.4 179.2 %copy-start.36 = (f32[768]{0:T(1024)S(1)}, f32[768]{0:T(1024)}, u32[]{:S(2)}) copy-start(f32[768]{0:T(1024)} %copy-done.35) | copy-start | bytes 9220
  1171.4 291.8 %all-gather.16.cloned.1.call-start = ((), (), s32[]{:S(2)}) async-start(), calls=%async_computation.20 | async-start | bytes 6144000 | tf_op jit(solution)/shard_map/all_gather | solution.py:38
  (66 other events, 685.5 us)
Sparse Core Ops, SparseCore 0:
  10.2 145.8 all-gather.7
  158.2 59.6 all-gather.9
  220.1 181.2 all-gather.11
  403.4 180.8 all-gather.13
  662.1 74.4 reduce-scatter.6
  740.1 213.6 reduce-scatter.8
  957.5 213.8 reduce-scatter.10
  1175.0 168.8 reduce-scatter.4
  1346.4 76.7 all-reduce.22
  1424.6 38.5 all-gather.15
